TPU v7x, 32 devices: a whole 2x2x4 slice. The times are simulated.
32 devices in a mesh: dp: 4 (over x, core), fsdp: 8 (over z, y).
Axes of the slice: x: 2, y: 2, z: 4, core: 2. Of those that a mesh axis runs over, the one named last changes fastest.
Arguments:
- tokens: bfloat16 [8192, 2048], P(('dp', 'fsdp')), may hold values from -6 to 6
- w_q: bfloat16 [2048, 2048], P(('dp', 'fsdp')), may hold values from -0.125 to 0.125
- w_kv: bfloat16 [2048, 256], P(('dp', 'fsdp')), may hold values from -0.125 to 0.125
- g_attn: bfloat16 [2048], P(('dp', 'fsdp')), may hold values from 0.25 to 1.75
- g_mlp: bfloat16 [2048], P(('dp', 'fsdp')), may hold values from 0.25 to 1.75
- w_o: bfloat16 [2048, 2048], P(('dp', 'fsdp')), may hold values from -0.75 to 0.75
- w_gu: bfloat16 [5632, 2, 2048], P(('dp', 'fsdp')), may hold values from -0.125 to 0.125
- w_down: bfloat16 [5632, 2048], P(('dp', 'fsdp')), may hold values from -0.078125 to 0.078125
- grad_out: bfloat16 [8192, 2048], P(('dp', 'fsdp')), may hold values from -6 to 6
- grad_kv: bfloat16 [8192, 256], P(('dp', 'fsdp')), may hold values from -4 to 4
- group_id: int32 [32], P(('dp', 'fsdp')), may hold values from 0 to 7
- group_size: int32 [8], replicated, may hold values from 1 to 4
- group_weight: float32 [8], replicated, may hold values from 1 to 4
Outputs:
- output: bfloat16 [8192, 2048], P(('dp', 'fsdp'))
- d_tokens: float32 [8192, 2048], P(('dp', 'fsdp'))
- kv_out: bfloat16 [8192, 256], P(('dp', 'fsdp'))
- d_kv: float32 [8192, 256], P(('dp', 'fsdp'))
- d_w_q: float32 [2048, 2048], P(('dp', 'fsdp'))
- d_w_kv: float32 [2048, 256], P(('dp', 'fsdp'))
- d_g_attn: float32 [2048], P(('dp', 'fsdp'))
- d_g_mlp: float32 [2048], P(('dp', 'fsdp'))
- d_w_o: float32 [2048, 2048], P(('dp', 'fsdp'))
- d_w_gu: float32 [5632, 2, 2048], P(('dp', 'fsdp'))
- d_w_down: float32 [5632, 2048], P(('dp', 'fsdp'))
All inputs are finite; a program needn't handle non-finite values.
Results may differ from a plain program's by a relative error of at most 0.015.
Values may be sent and summed in bfloat16 or wider, within the bound.
No kernel may reach another device: no remote copies, remote signals or barrier semaphores. Data moves between devices by JAX's collectives and lax.ppermute only.
A program may use at most 256 MiB of HBM per device.

v0:
```python
import jax
import jax.numpy as jnp
from jax import lax
from jax.sharding import PartitionSpec as P

epsilon = 1e-05
theta_base = 10000.0


def rope_tables(length, width):
    halfway = width // 2
    freqs = theta_base ** (-(jnp.arange(halfway, dtype=jnp.float32) * 2.0 / width))
    angles = jnp.arange(length, dtype=jnp.float32)[:, None] * freqs[None, :]
    return (jnp.cos(angles), jnp.sin(angles))


def rotate(vectors, cosines, sine_part):
    halfway = vectors.shape[-1] // 2
    front = vectors[..., :halfway]
    behind = vectors[..., halfway:]
    return jnp.concatenate(
        [front * cosines - behind * sine_part, behind * cosines + front * sine_part], axis=-1
    )


def contract_last(left, right):
    return lax.dot_general(
        left,
        right,
        (((left.ndim - 1,), (right.ndim - 1,)), ((), ())),
        preferred_element_type=jnp.float32,
    )


def contract_first(left, right):
    return lax.dot_general(
        left, right, (((0,), (0,)), ((), ())), preferred_element_type=jnp.float32
    )


def local(
    tokens,
    w_q,
    w_kv,
    g_attn,
    g_mlp,
    w_o,
    w_gu,
    w_down,
    grad_out,
    grad_kv,
    group_id,
    group_size,
    group_weight,
):
    length, width = tokens.shape
    head_dim = grad_kv.shape[1] // 2
    q_width = w_q.shape[1]
    head_count = q_width // head_dim
    matches = jnp.arange(group_size.shape[0], dtype=jnp.int32) == group_id[0]
    factor = jnp.sum(jnp.where(matches, group_weight / group_size.astype(jnp.float32), 0.0))
    cosines, sine_part = rope_tables(length, head_dim)
    x_full = tokens.astype(jnp.float32)
    inv_one = lax.rsqrt(jnp.mean(x_full * x_full, axis=-1, keepdims=True) + epsilon)
    normed_one = x_full * inv_one
    wq_piece = lax.all_gather(w_q, ("dp", "fsdp"), axis=0, tiled=True)
    wkv_piece = lax.all_gather(w_kv, ("dp", "fsdp"), axis=0, tiled=True)
    gain_piece = lax.all_gather(g_attn, ("dp", "fsdp"), axis=0, tiled=True)
    mlp_gain_piece = lax.all_gather(g_mlp, ("dp", "fsdp"), axis=0, tiled=True)
    normed_cols = normed_one
    h_cols = (normed_cols * gain_piece.astype(jnp.float32)).astype(jnp.bfloat16)
    q_acc = jnp.dot(h_cols, wq_piece, preferred_element_type=jnp.float32)
    kv_acc = jnp.dot(h_cols, wkv_piece, preferred_element_type=jnp.float32)
    gain_two = mlp_gain_piece.astype(jnp.float32)
    q_pre, kv_pre, gain_two, h_one = (q_acc, kv_acc, gain_two, h_cols)
    q_low = rotate(
        q_pre.reshape(length, head_count, head_dim), cosines[:, None, :], sine_part[:, None, :]
    ).astype(jnp.bfloat16)
    k_low = rotate(kv_pre[:, :head_dim], cosines, sine_part).astype(jnp.bfloat16)
    v_low = kv_pre[:, head_dim:].astype(jnp.bfloat16)
    score_scale = head_dim ** (-0.5)
    causal = jnp.arange(length)[:, None] >= jnp.arange(length)[None, :]

    def logits_of(queries, keys):
        raw_scores = jnp.einsum("thd,sd->hts", queries, keys, preferred_element_type=jnp.float32)
        return jnp.where(causal[None], raw_scores * score_scale, -1e30)

    logits = logits_of(q_low, k_low)
    row_top = jnp.max(logits, axis=-1, keepdims=True)
    exp_vals = jnp.exp(logits - row_top)
    row_total = jnp.sum(exp_vals, axis=-1, keepdims=True)
    prob_full = exp_vals / row_total
    log_total = row_top + jnp.log(row_total)
    prob_low = prob_full.astype(jnp.bfloat16)
    attended = jnp.einsum("hts,sd->thd", prob_low, v_low, preferred_element_type=jnp.float32)
    attn_low = attended.reshape(length, q_width).astype(jnp.bfloat16)
    branch = jnp.dot(
        attn_low,
        lax.all_gather(w_o, ("dp", "fsdp"), axis=0, tiled=True),
        preferred_element_type=jnp.float32,
    )
    x_mid = x_full + branch
    inv_two = lax.rsqrt(jnp.mean(x_mid * x_mid, axis=-1, keepdims=True) + epsilon)
    normed_two = x_mid * inv_two
    h_two = (normed_two * gain_two).astype(jnp.bfloat16)
    grad_top = grad_out.astype(jnp.float32) * factor
    grad_low = grad_top.astype(jnp.bfloat16)
    ff_rows, grad_rows = (
        lax.all_gather(h_two, "dp", axis=0, tiled=True),
        lax.all_gather(grad_low, "dp", axis=0, tiled=True),
    )
    gu_piece = lax.all_gather(w_gu, "fsdp", axis=0, tiled=True)
    down_piece = lax.all_gather(w_down, "fsdp", axis=0, tiled=True)
    both_proj = jnp.einsum("td,fkd->tkf", ff_rows, gu_piece, preferred_element_type=jnp.float32)
    gate_vals = both_proj[:, 0]
    up_vals = both_proj[:, 1]
    hid_cols = (jax.nn.silu(gate_vals) * up_vals).astype(jnp.bfloat16)
    mlp_out = jnp.dot(hid_cols, down_piece, preferred_element_type=jnp.float32)
    mlp_part = mlp_out
    gate_all = gate_vals
    up_all = up_vals
    mlp_out = lax.psum_scatter(
        mlp_part.astype(jnp.bfloat16), "dp", scatter_dimension=0, tiled=True
    ).astype(jnp.float32)
    gu_piece = lax.all_gather(w_gu, "fsdp", axis=0, tiled=True)
    down_piece = lax.all_gather(w_down, "fsdp", axis=0, tiled=True)
    gate_vals = gate_all
    up_vals = up_all
    d_hid = contract_last(grad_rows, down_piece)
    sigmoid_vals = jax.nn.sigmoid(gate_vals)
    d_gate = d_hid * up_vals * sigmoid_vals * (1.0 + gate_vals * (1.0 - sigmoid_vals))
    d_up = d_hid * gate_vals * sigmoid_vals
    d_both = jnp.stack([d_gate, d_up], axis=1).astype(jnp.bfloat16)
    d_h_two = jnp.einsum("tkf,fkd->td", d_both, gu_piece, preferred_element_type=jnp.float32)
    d_h_part = d_h_two
    d_h_two = lax.psum_scatter(
        d_h_part.astype(jnp.bfloat16), "dp", scatter_dimension=0, tiled=True
    ).astype(jnp.float32)
    d_w_down = lax.psum_scatter(
        contract_first(hid_cols, grad_rows).astype(jnp.bfloat16),
        "fsdp",
        scatter_dimension=0,
        tiled=True,
    ).astype(jnp.float32)
    d_w_gu = lax.psum_scatter(
        jnp.einsum("tkf,td->fkd", d_both, ff_rows, preferred_element_type=jnp.float32).astype(
            jnp.bfloat16
        ),
        "fsdp",
        scatter_dimension=0,
        tiled=True,
    ).astype(jnp.float32)
    output = (x_mid + mlp_out).astype(jnp.bfloat16)
    d_gain_two = jnp.sum(d_h_two * normed_two, axis=0)
    d_normed_two = d_h_two * gain_two
    d_mid = grad_top + inv_two * (
        d_normed_two - normed_two * jnp.mean(d_normed_two * normed_two, axis=-1, keepdims=True)
    )
    d_mid_low = d_mid.astype(jnp.bfloat16)
    d_attended = contract_last(d_mid_low, lax.all_gather(w_o, ("dp", "fsdp"), axis=0, tiled=True))
    d_att_low = d_attended.astype(jnp.bfloat16).reshape(length, head_count, head_dim)
    d_w_o = lax.psum_scatter(
        contract_first(attn_low, d_mid_low), ("dp", "fsdp"), scatter_dimension=0, tiled=True
    )
    prob_back = jnp.exp(logits_of(q_low, k_low) - log_total)
    prob_back_low = prob_back.astype(jnp.bfloat16)
    d_probs = jnp.einsum("thd,sd->hts", d_att_low, v_low, preferred_element_type=jnp.float32)
    d_v_own = jnp.einsum(
        "hts,thd->sd", prob_back_low, d_att_low, preferred_element_type=jnp.float32
    )
    d_logit = prob_back * (d_probs - jnp.sum(prob_back * d_probs, axis=-1, keepdims=True))
    d_raw = (d_logit * score_scale).astype(jnp.bfloat16)
    d_q_rot = jnp.einsum("hts,sd->thd", d_raw, k_low, preferred_element_type=jnp.float32)
    d_k_own = jnp.einsum("hts,thd->sd", d_raw, q_low, preferred_element_type=jnp.float32)
    kv_extra = grad_kv.astype(jnp.float32) * factor
    d_k_total = d_k_own + kv_extra[:, :head_dim]
    d_v_total = d_v_own + kv_extra[:, head_dim:]
    d_kv = jnp.concatenate([d_k_total, d_v_total], axis=1)
    d_kv_low = jnp.concatenate([rotate(d_k_total, cosines, -sine_part), d_v_total], axis=1).astype(
        jnp.bfloat16
    )
    d_q_low = (
        rotate(d_q_rot, cosines[:, None, :], -sine_part[:, None, :])
        .reshape(length, q_width)
        .astype(jnp.bfloat16)
    )
    wq_piece = lax.all_gather(w_q, ("dp", "fsdp"), axis=0, tiled=True)
    wkv_piece = lax.all_gather(w_kv, ("dp", "fsdp"), axis=0, tiled=True)
    gain_piece = lax.all_gather(g_attn, ("dp", "fsdp"), axis=0, tiled=True)
    d_h_cols = contract_last(d_q_low, wq_piece) + contract_last(d_kv_low, wkv_piece)
    normed_cols = normed_one
    d_normed = d_h_cols * gain_piece.astype(jnp.float32)
    d_gain = jnp.sum(d_h_cols * normed_cols, axis=0)
    d_tokens = d_mid + inv_one * (
        d_normed - normed_one * jnp.mean(d_normed * normed_one, axis=-1, keepdims=True)
    )
    joined = jnp.concatenate([d_q_low, d_kv_low], axis=1)
    d_w_in = lax.psum_scatter(
        contract_first(h_one, joined), ("dp", "fsdp"), scatter_dimension=0, tiled=True
    )
    d_g_attn, d_g_mlp = (
        lax.psum_scatter(d_gain, ("dp", "fsdp"), scatter_dimension=0, tiled=True),
        lax.psum_scatter(d_gain_two, ("dp", "fsdp"), scatter_dimension=0, tiled=True),
    )
    kv_out = jnp.concatenate([k_low, v_low], axis=1)
    return (
        output,
        d_tokens,
        kv_out,
        d_kv,
        d_w_in[:, :q_width],
        d_w_in[:, q_width:],
        d_g_attn,
        d_g_mlp,
        d_w_o,
        d_w_gu,
        d_w_down,
    )


def solution(mesh):
    placed = (
        P(("dp", "fsdp"), None),
        P(("dp", "fsdp"), None),
        P(("dp", "fsdp"), None),
        P(("dp", "fsdp")),
        P(("dp", "fsdp")),
        P(("dp", "fsdp"), None),
        P(("dp", "fsdp"), None, None),
        P(("dp", "fsdp"), None),
        P(("dp", "fsdp"), None),
        P(("dp", "fsdp"), None),
        P(("dp", "fsdp")),
        P(),
        P(),
    )
    return jax.shard_map(
        local,
        mesh=mesh,
        in_specs=placed,
        out_specs=(
            P(("dp", "fsdp"), None),
            P(("dp", "fsdp"), None),
            P(("dp", "fsdp"), None),
            P(("dp", "fsdp"), None),
            P(("dp", "fsdp"), None),
            P(("dp", "fsdp"), None),
            P(("dp", "fsdp")),
            P(("dp", "fsdp")),
            P(("dp", "fsdp"), None),
            P(("dp", "fsdp"), None, None),
            P(("dp", "fsdp"), None),
        ),
        check_vma=False,
    )
```

profile of v0, /device:TPU:0, one launch (start us, length us, event | category | flops | bytes accessed | tf_op | source)
XLA Modules:
  0.0 1734.8 jit_solution(2765132462502652689)
XLA Ops:
  13.1 42.2 %all-reduce.6 = (bf16[2048]{0:T(1024)(128)(2,1)S(1)}, bf16[2048]{0:T(1024)(128)(2,1)S(1)}) all-reduce(bf16[2048]{0:T(1024)(128)(2,1)S(1)} %dynamic-update-slice, bf16[2048]{0:T(1024)(128)(2,1)S(1)} %dynamic-update-slice.1), channel_id=1, replica_groups=mesh['dp'=4,'fsdp'=8] {'dp','fsdp'}, use_global_device_ids=true, to_apply=%add | all-reduce | flops 4096 | bytes 16384
  55.6 12.1 all-gather.8.cloned.1.call-done
  70.2 76.8 %all-gather.10.cloned.1.call-done = bf16[2048,2048]{1,0:T(8,128)(2,1)} async-done(((bf16[64,2048]{1,0:T(8,128)(2,1)}), bf16[2048,2048]{1,0:T(8,128)(2,1)}) %all-gather.10.cloned.1.call-update) | async-done | bytes 8388624 | tf_op jit(solution)/shard_map/all_gather | solution.py:66
  147.0 5.8 convolution_bitcast_fusion.1
  160.6 65.3 %all-gather.12.cloned.1.call-done = bf16[2048,2048]{1,0:T(8,128)(2,1)} async-done(((bf16[64,2048]{1,0:T(8,128)(2,1)}), bf16[2048,2048]{1,0:T(8,128)(2,1)}) %all-gather.12.cloned.1.call-update) | async-done | bytes 8388624 | tf_op jit(solution)/shard_map/all_gather | solution.py:99
  225.9 6.2 multiply_reduce_fusion
  239.1 151.7 %all-gather.16.cloned.1.call-done = bf16[1408,2,2048]{2,0,1:T(8,128)(2,1)} async-done(((bf16[176,2,2048]{2,0,1:T(8,128)(2,1)}), bf16[1408,2,2048]{2,0,1:T(8,128)(2,1)}) %all-gather.16.cloned.1.call-update) | async-done | bytes 11534352 | tf_op jit(solution)/shard_map/all_gather | solution.py:112
  390.8 34.7 %all-gather.14.cloned.1.call-done = bf16[1024,2048]{1,0:T(8,128)(2,1)} async-done(((bf16[256,2048]{1,0:T(8,128)(2,1)}), bf16[1024,2048]{1,0:T(8,128)(2,1)}) %all-gather.14.cloned.1.call-update) | async-done | bytes 4194320 | tf_op jit(solution)/shard_map/all_gather | solution.py:109
  425.5 18.8 %convolution_bitcast_fusion = f32[1024,2,1408]{2,0,1:T(8,128)} fusion(bf16[1408,2,2048]{2,0,1:T(8,128)(2,1)} %all-gather.16.cloned.1.call-done, bf16[1024,2048]{1,0:T(8,128)(2,1)} %all-gather.14.cloned.1.call-done), kind=kOutput, calls=%fused_computation.4 | convolution fusion | flops 11811160064 | bytes 27262976 | tf_op jit(solution)/shard_map/td,fkd->tkf/dot_general | solution.py:114
  444.3 17.7 %all-gather.20.cloned.1.call-done = bf16[1024,2048]{1,0:T(8,128)(2,1)} async-done(((bf16[256,2048]{1,0:T(8,128)(2,1)}), bf16[1024,2048]{1,0:T(8,128)(2,1)}) %all-gather.20.cloned.1.call-update) | async-done | bytes 4194320 | tf_op jit(solution)/shard_map/all_gather | solution.py:110
  462.0 94.9 %all-gather.18.cloned.1.call-done = bf16[1408,2048]{1,0:T(8,128)(2,1)} async-done(((bf16[176,2048]{1,0:T(8,128)(2,1)}), bf16[1408,2048]{1,0:T(8,128)(2,1)}) %all-gather.18.cloned.1.call-update) | async-done | bytes 5767184 | tf_op jit(solution)/shard_map/all_gather | solution.py:113
  556.9 15.6 fusion.13
  575.0 16.3 bitcast_convert_fusion
  591.6 10.9 convolution_convert_fusion.1
  602.6 10.5 convolution_convert_fusion
  613.2 18.3 %convert_bitcast_fusion = bf16[1408,2,2048]{0,2,1:T(8,128)(2,1)} fusion(bf16[1024,2048]{1,0:T(8,128)(2,1)} %all-gather.14.cloned.1.call-done, bf16[1024,1,1408]{2,0,1:T(8,128)(2,1)} %copy-done.31, bf16[1024,1,1408]{2,0,1:T(8,128)(2,1)} %copy-done.30), kind=kOutput, calls=%fused_computation.1 | convolution fusion | flops 11828461568 | bytes 21495808 | tf_op jit(solution)/shard_map/tkf,td->fkd/dot_general | solution.py:146
  631.6 29.4 %copy.89 = bf16[1408,2,2048]{2,1,0:T(2,128)(2,1)} copy(bf16[1408,2,2048]{0,2,1:T(8,128)(2,1)} %convert_bitcast_fusion) | data formatting | bytes 23068672 | tf_op jit(solution)/shard_map/convert_element_type | solution.py:146
  668.8 12.7 reduce-scatter.6.cloned.1.call-done
  681.5 4.4 fusion.18
  687.3 5.7 convolution_convert_fusion.2
  697.2 9.2 fusion.49
  707.8 9.5 fusion.35
  723.5 4.1 fusion.85
  727.6 8.2 fusion.37
  737.4 9.3 fusion.53
  752.2 6.2 fusion.88
  760.6 42.5 %all-reduce.5 = (f32[2048]{0:T(1024)S(1)}, f32[2048]{0:T(1024)S(1)}) all-reduce(f32[2048]{0:T(1024)S(1)} %get-tuple-element.46, f32[2048]{0:T(1024)S(1)} %copy-done.21), channel_id=5, replica_groups=mesh['dp'=4,'fsdp'=8] {'dp','fsdp'}, use_global_device_ids=true, to_apply=%region_12.13.clone | all-reduce | flops 4096 | bytes 32768
  804.3 4.1 fusion.24
  810.8 345.1 %all-reduce.9.cloned.1.call-done = bf16[1408,2,2048]{2,1,0:T(2,128)(2,1)} async-done(((bf16[1408,2,2048]{2,1,0:T(2,128)(2,1)}), bf16[1408,2,2048]{2,1,0:T(2,128)(2,1)}) %all-reduce.9.cloned.1.call-update) | async-done | bytes 11534352
  1155.9 4.6 dynamic-slice_convert_fusion
  1160.5 207.4 %reduce-scatter.10.cloned.1.call-done = f32[64,2304]{1,0:T(8,128)} async-done(((f32[2048,2304]{1,0:T(8,128)}), f32[64,2304]{1,0:T(8,128)}) %reduce-scatter.10.cloned.1.call-update) | async-done | bytes 589840 | tf_op jit(solution)/shard_map/reduce_scatter | solution.py:198
  1371.3 356.5 %reduce-scatter.12.cloned.1.call-done = f32[64,2048]{1,0:T(8,128)} async-done(((f32[2048,2048]{1,0:T(8,128)}), f32[64,2048]{1,0:T(8,128)}) %reduce-scatter.12.cloned.1.call-update) | async-done | bytes 524304 | tf_op jit(solution)/shard_map/reduce_scatter | solution.py:162
  (142 shorter events, 61.7 us)
Async XLA Ops:
  7.2 5.4 copy-start.27
  7.2 5.7 copy-start.28
  7.2 48.1 %copy-start.1 = (bf16[256,2048]{1,0:T(8,128)(2,1)S(1)}, bf16[256,2048]{1,0:T(8,128)(2,1)}, u32[]{:S(2)}) copy-start(bf16[256,2048]{1,0:T(8,128)(2,1)} %param.13) | copy-start | bytes 3145732
  7.2 60.6 %all-gather.8.cloned.1.call-start = ((), (), s32[]{:S(2)}) async-start(), calls=%async_computation.5 | async-start | bytes 1081344 | tf_op jit(solution)/shard_map/all_gather | solution.py:67
  7.9 139.1 %all-gather.10.cloned.1.call-start = ((), (), s32[]{:S(2)}) async-start(), calls=%async_computation.6 | async-start | bytes 8650752 | tf_op jit(solution)/shard_map/all_gather | solution.py:66
  8.7 217.2 %all-gather.12.cloned.1.call-start = ((), (), s32[]{:S(2)}) async-start(), calls=%async_computation.7 | async-start | bytes 8650752 | tf_op jit(solution)/shard_map/all_gather | solution.py:99
  9.4 381.4 %all-gather.16.cloned.1.call-start = ((), (), s32[]{:S(2)}) async-start(), calls=%async_computation.9 | async-start | bytes 12976128 | tf_op jit(solution)/shard_map/all_gather | solution.py:112
  12.5 413.0 %all-gather.14.cloned.1.call-start = ((), (), s32[]{:S(2)}) async-start(), calls=%async_computation.8 | async-start | bytes 5242880 | tf_op jit(solution)/shard_map/all_gather | solution.py:109
  55.3 14.7 copy-start.23
  55.6 97.2 %copy-start.19 = (f32[256]{0:T(256)}, f32[256]{0:T(256)S(1)}, u32[]{:S(2)}) copy-start(f32[256]{0:T(256)S(1)} %add_rsqrt_fusion.1) | copy-start | bytes 3076
  69.6 87.6 %copy-start.11 = (f32[256,256]{0,1:T(8,128)}, f32[256,256]{0,1:T(8,128)S(1)}, u32[]{:S(2)}) copy-start(f32[256,256]{0,1:T(8,128)S(1)} %fusion.81) | copy-start | bytes 786436
  70.0 85.3 %copy-start.12 = (bf16[256,64]{0,1:T(8,128)(2,1)}, bf16[256,64]{0,1:T(8,128)(2,1)S(1)}, u32[]{:S(2)}) copy-start(bf16[256,64]{0,1:T(8,128)(2,1)S(1)} %get-tuple-element.63) | copy-start | bytes 98308
  70.0 85.3 %copy-start.14 = (bf16[256,64]{0,1:T(8,128)(2,1)}, bf16[256,64]{0,1:T(8,128)(2,1)S(1)}, u32[]{:S(2)}) copy-start(bf16[256,64]{0,1:T(8,128)(2,1)S(1)} %get-tuple-element.64) | copy-start | bytes 98308
  156.7 4.0 copy-start.16
  232.1 5.8 copy-start.22
  233.4 228.6 %all-gather.20.cloned.1.call-start = ((), (), s32[]{:S(2)}) async-start(), calls=%async_computation.12 | async-start | bytes 5242880 | tf_op jit(solution)/shard_map/all_gather | solution.py:110
  237.9 318.9 %all-gather.18.cloned.1.call-start = ((), (), s32[]{:S(2)}) async-start(), calls=%async_computation.10 | async-start | bytes 6488064 | tf_op jit(solution)/shard_map/all_gather | solution.py:113
  238.7 427.0 %reduce-scatter.8.cloned.1.call-start = ((), (), s32[]{:S(2)}) async-start(), calls=%async_computation.13 | async-start | bytes 5242880 | tf_op jit(solution)/shard_map/reduce_scatter | solution.py:136
  591.4 90.1 %reduce-scatter.6.cloned.1.call-start = ((), (), s32[]{:S(2)}) async-start(), calls=%async_computation.11 | async-start | bytes 5242880 | tf_op jit(solution)/shard_map/reduce_scatter | solution.py:122
  602.6 205.8 %reduce-scatter.14.cloned.1.call-start = ((), (), s32[]{:S(2)}) async-start(), calls=%async_computation.16 | async-start | bytes 6488064 | tf_op jit(solution)/shard_map/reduce_scatter | solution.py:139
  613.2 542.7 %all-reduce.9.cloned.1.call-start = ((), (), s32[]{:S(2)}) async-start(), calls=%async_computation.17 | async-start | bytes 23068672
  661.0 706.9 %reduce-scatter.10.cloned.1.call-start = ((), (), s32[]{:S(2)}) async-start(), calls=%async_computation.14 | async-start | bytes 19464192 | tf_op jit(solution)/shard_map/reduce_scatter | solution.py:198
  664.2 33.0 %copy-start.9 = (f32[256,256]{0,1:T(8,128)}, f32[256,256]{0,1:T(8,128)S(1)}, u32[]{:S(2)}) copy-start(f32[256,256]{0,1:T(8,128)S(1)} %convert_multiply_fusion.5) | copy-start | bytes 786436
  693.5 3.7 copy-start.5
  697.2 9.3 copy-start.24
  720.4 3.1 copy-start.10
  723.5 12.3 copy-start.7
  723.5 4.1 copy-start.20
  735.8 992.0 %reduce-scatter.12.cloned.1.call-start = ((), (), s32[]{:S(2)}) async-start(), calls=%async_computation.15 | async-start | bytes 17301504 | tf_op jit(solution)/shard_map/reduce_scatter | solution.py:162
  746.7 2.8 copy-start.13
  746.7 2.8 copy-start.15
  752.2 6.2 copy-start.8
  (13 other events, 21.6 us)
Sparse Core Ops, SparseCore 0:
  11.1 56.5 all-gather.7
  70.7 76.2 all-gather.9
  150.0 75.8 all-gather.11
  228.5 162.2 all-gather.15
  392.8 32.6 all-gather.13
  427.5 34.4 all-gather.19
  464.2 92.6 all-gather.17
  591.5 42.6 reduce-scatter.7
  636.9 44.5 reduce-scatter.5
  685.0 111.5 reduce-scatter.13
  800.5 355.3 all-reduce.8
  1162.1 205.7 reduce-scatter.9
  1370.8 356.9 reduce-scatter.11
where the time goes:
time: 1750 us; the launch traced here: 1730 us
  waiting for transfers between devices  1380 us (79%)
  matrix products  166 us (9%)
  blocking collectives  84.7 us (5%)
  local copies, waits for them, and re-layouts  52.5 us (3%)
  other arithmetic  36.2 us (2%)
    reduce_scatter x1, waiting for transfers between devices, local(): lax.psum_scatter(contract_first(attn_low, d_mid_low), ('dp', 'fsdp'), sca...  357 us
    unnamed x14, waiting for transfers between devices  348 us
    reduce_scatter x1, waiting for transfers between devices, local(): lax.psum_scatter(contract_first(h_one, joined), ('dp', 'fsdp'), scatter_d...  207 us
    all_gather x1, waiting for transfers between devices, local(): gu_piece = lax.all_gather(w_gu, 'fsdp', axis=0, tiled=True)  152 us
    all_gather x1, waiting for transfers between devices, local(): down_piece = lax.all_gather(w_down, 'fsdp', axis=0, tiled=True)  94.9 us
    unnamed x2, blocking collectives  84.7 us
    all_gather x1, waiting for transfers between devices, local(): wq_piece = lax.all_gather(w_q, ('dp', 'fsdp'), axis=0, tiled=True)  76.8 us
    all_gather x1, waiting for transfers between devices, local(): lax.all_gather(w_o, ('dp', 'fsdp'), axis=0, tiled=True)  65.3 us
  transfers between devices with their start and end apart: 13, of which 11 were waited for; matrix products, arithmetic and copies ran while one was open for 12% of the time, Pallas kernels for 0%

commit v1 on v0

--- a/solution.py
+++ b/solution.py
@@ -5,6 +5,24 @@
 
 epsilon = 1e-05
 theta_base = 10000.0
+
+
+def gather_around(shard, axis, dim):
+    ways, here, hop = (lax.axis_size(axis), lax.axis_index(axis), shard.shape[dim])
+    shape = [n * ways if d == dim else n for d, n in enumerate(shard.shape)]
+    full = lax.dynamic_update_slice_in_dim(
+        jnp.zeros(shape, shard.dtype), shard, here * hop, axis=dim
+    )
+    going_up = going_down = shard
+    for far in range(1, ways // 2 + 1):
+        going_up = lax.ppermute(going_up, axis, [(d, (d + 1) % ways) for d in range(ways)])
+        full = lax.dynamic_update_slice_in_dim(full, going_up, (here - far) % ways * hop, axis=dim)
+        if 2 * far < ways:
+            going_down = lax.ppermute(going_down, axis, [(d, (d - 1) % ways) for d in range(ways)])
+            full = lax.dynamic_update_slice_in_dim(
+                full, going_down, (here + far) % ways * hop, axis=dim
+            )
+    return full
 
 
 def rope_tables(length, width):
@@ -110,7 +128,7 @@
         lax.all_gather(grad_low, "dp", axis=0, tiled=True),
     )
     gu_piece = lax.all_gather(w_gu, "fsdp", axis=0, tiled=True)
-    down_piece = lax.all_gather(w_down, "fsdp", axis=0, tiled=True)
+    down_piece = gather_around(w_down, "fsdp", 0)
     both_proj = jnp.einsum("td,fkd->tkf", ff_rows, gu_piece, preferred_element_type=jnp.float32)
     gate_vals = both_proj[:, 0]
     up_vals = both_proj[:, 1]

time: 1750 us -> 1820 us (1.040)
  waiting for transfers between devices: 1380 us -> 1440 us
    ppermute x0 -> x7, waiting for transfers between devices: none -> 92.4 us  [the longest x4 92 us: gather_around(): lax.ppermute(going_up, axis, [(d, (d + 1) % ways) for d in range(ways)])]
    unnamed x14, waiting for transfers between devices: 348 us -> 326 us
  transfers between devices with their start and end apart: 13 -> 20, of which waited for: 11 -> 15; matrix products, arithmetic and copies ran while one was open for 12% -> 12% of each run, Pallas kernels for 0% -> 0%
where the time goes in v1:
time: 1820 us; the launch traced here: 1810 us
  waiting for transfers between devices  1440 us (79%)
  matrix products  165 us (9%)
  blocking collectives  81.5 us (4%)
  local copies, waits for them, and re-layouts  58.4 us (3%)
  other arithmetic  35.3 us (2%)
  starting transfers between devices  18.2 us (1%)
    reduce_scatter x1, waiting for transfers between devices, local(): lax.psum_scatter(contract_first(attn_low, d_mid_low), ('dp', 'fsdp'), sca...  357 us
    unnamed x14, waiting for transfers between devices  326 us
    reduce_scatter x1, waiting for transfers between devices, local(): lax.psum_scatter(contract_first(h_one, joined), ('dp', 'fsdp'), scatter_d...  207 us
    all_gather x1, waiting for transfers between devices, local(): gu_piece = lax.all_gather(w_gu, 'fsdp', axis=0, tiled=True)  152 us
    all_gather x1, waiting for transfers between devices, local(): down_piece = lax.all_gather(w_down, 'fsdp', axis=0, tiled=True)  94.9 us
    ppermute x4, waiting for transfers between devices, gather_around(): lax.ppermute(going_up, axis, [(d, (d + 1) % ways) for d in range(ways)])  92 us
    unnamed x2, blocking collectives  81.5 us
    all_gather x1, waiting for transfers between devices, local(): wq_piece = lax.all_gather(w_q, ('dp', 'fsdp'), axis=0, tiled=True)  76.8 us
  transfers between devices with their start and end apart: 20, of which 15 were waited for; matrix products, arithmetic and copies ran while one was open for 12% of the time, Pallas kernels for 0%

profile of v1, /device:TPU:0, one launch (start us, length us, event | category | flops | bytes accessed | tf_op | source)
XLA Modules:
  0.0 1809.9 jit_solution(4096346867762497731)
XLA Ops:
  13.1 42.1 %all-reduce.6 = (bf16[2048]{0:T(1024)(128)(2,1)S(1)}, bf16[2048]{0:T(1024)(128)(2,1)S(1)}) all-reduce(bf16[2048]{0:T(1024)(128)(2,1)S(1)} %dynamic-update-slice, bf16[2048]{0:T(1024)(128)(2,1)S(1)} %dynamic-update-slice.1), channel_id=1, replica_groups=mesh['dp'=4,'fsdp'=8] {'dp','fsdp'}, use_global_device_ids=true, to_apply=%add | all-reduce | flops 4096 | bytes 16384
  56.2 11.6 all-gather.8.cloned.1.call-done
  70.2 76.8 %all-gather.10.cloned.1.call-done = bf16[2048,2048]{1,0:T(8,128)(2,1)} async-done(((bf16[64,2048]{1,0:T(8,128)(2,1)}), bf16[2048,2048]{1,0:T(8,128)(2,1)}) %all-gather.10.cloned.1.call-update) | async-done | bytes 8388624 | tf_op jit(solution)/shard_map/all_gather | solution.py:84
  147.0 5.8 convolution_bitcast_fusion.1
  160.6 65.4 %all-gather.12.cloned.1.call-done = bf16[2048,2048]{1,0:T(8,128)(2,1)} async-done(((bf16[64,2048]{1,0:T(8,128)(2,1)}), bf16[2048,2048]{1,0:T(8,128)(2,1)}) %all-gather.12.cloned.1.call-update) | async-done | bytes 8388624 | tf_op jit(solution)/shard_map/all_gather | solution.py:117
  226.1 6.2 multiply_reduce_fusion
  238.9 152.1 %all-gather.16.cloned.1.call-done = bf16[1408,2,2048]{2,0,1:T(8,128)(2,1)} async-done(((bf16[176,2,2048]{2,0,1:T(8,128)(2,1)}), bf16[1408,2,2048]{2,0,1:T(8,128)(2,1)}) %all-gather.16.cloned.1.call-update) | async-done | bytes 11534352 | tf_op jit(solution)/shard_map/all_gather | solution.py:130
  390.9 34.7 %all-gather.14.cloned.1.call-done = bf16[1024,2048]{1,0:T(8,128)(2,1)} async-done(((bf16[256,2048]{1,0:T(8,128)(2,1)}), bf16[1024,2048]{1,0:T(8,128)(2,1)}) %all-gather.14.cloned.1.call-update) | async-done | bytes 4194320 | tf_op jit(solution)/shard_map/all_gather | solution.py:127
  425.6 19.2 %convolution_bitcast_fusion = f32[1024,2,1408]{2,0,1:T(8,128)} fusion(bf16[1408,2,2048]{2,0,1:T(8,128)(2,1)} %all-gather.16.cloned.1.call-done, bf16[1024,2048]{1,0:T(8,128)(2,1)} %all-gather.14.cloned.1.call-done), kind=kOutput, calls=%fused_computation.4 | convolution fusion | flops 11811160064 | bytes 27262976 | tf_op jit(solution)/shard_map/td,fkd->tkf/dot_general | solution.py:132
  444.8 17.3 all-gather.18.cloned.1.call-done
  462.1 94.9 %all-gather.20.cloned.1.call-done = bf16[1408,2048]{1,0:T(8,128)(2,1)} async-done(((bf16[176,2048]{1,0:T(8,128)(2,1)}), bf16[1408,2048]{1,0:T(8,128)(2,1)}) %all-gather.20.cloned.1.call-update) | async-done | bytes 5767184 | tf_op jit(solution)/shard_map/all_gather | solution.py:144
  557.0 15.6 fusion.13
  575.1 16.3 bitcast_convert_fusion
  596.6 26.3 %collective-permute-done = bf16[176,2048]{1,0:T(8,128)(2,1)} collective-permute-done((bf16[176,2048]{1,0:T(8,128)(2,1)}, bf16[176,2048]{1,0:T(8,128)(2,1)}, u32[]{:S(2)}, u32[]{:S(2)}) %collective-permute-start) | collective-permute-done | bytes 720928 | tf_op jit(solution)/shard_map/ppermute | solution.py:18
  628.5 26.8 %collective-permute-done.2 = bf16[176,2048]{1,0:T(8,128)(2,1)} collective-permute-done((bf16[176,2048]{1,0:T(8,128)(2,1)}, bf16[176,2048]{1,0:T(8,128)(2,1)}, u32[]{:S(2)}, u32[]{:S(2)}) %collective-permute-start.2) | collective-permute-done | bytes 720928 | tf_op jit(solution)/shard_map/ppermute | solution.py:18
  664.0 23.6 %collective-permute-done.4 = bf16[176,2048]{1,0:T(8,128)(2,1)S(1)} collective-permute-done((bf16[176,2048]{1,0:T(8,128)(2,1)}, bf16[176,2048]{1,0:T(8,128)(2,1)S(1)}, u32[]{:S(2)}, u32[]{:S(2)}) %collective-permute-start.4) | collective-permute-done | bytes 720928 | tf_op jit(solution)/shard_map/ppermute | solution.py:18
  690.6 15.3 collective-permute-done.6
  706.0 8.3 convolution_convert_fusion.1
  714.4 10.5 convolution_convert_fusion
  725.2 18.3 %convert_bitcast_fusion = bf16[1408,2,2048]{0,2,1:T(8,128)(2,1)} fusion(bf16[1024,2048]{1,0:T(8,128)(2,1)} %all-gather.14.cloned.1.call-done, bf16[1024,1,1408]{2,0,1:T(8,128)(2,1)} %copy-done.36, bf16[1024,1,1408]{2,0,1:T(8,128)(2,1)} %copy-done.35), kind=kOutput, calls=%fused_computation.1 | convolution fusion | flops 11828461568 | bytes 21495808 | tf_op jit(solution)/shard_map/tkf,td->fkd/dot_general | solution.py:164
  743.5 29.2 %copy.89 = bf16[1408,2,2048]{2,1,0:T(2,128)(2,1)} copy(bf16[1408,2,2048]{0,2,1:T(8,128)(2,1)} %convert_bitcast_fusion) | data formatting | bytes 23068672 | tf_op jit(solution)/shard_map/convert_element_type | solution.py:164
  785.6 6.8 convolution_convert_fusion.2
  797.8 9.3 fusion.49
  808.4 9.5 fusion.35
  828.2 8.1 fusion.37
  837.9 9.6 fusion.53
  853.0 6.2 fusion.88
  861.5 39.4 %all-reduce.5 = (f32[2048]{0:T(1024)S(1)}, f32[2048]{0:T(1024)S(1)}) all-reduce(f32[2048]{0:T(1024)S(1)} %get-tuple-element.46, f32[2048]{0:T(1024)S(1)} %copy-done.26), channel_id=5, replica_groups=mesh['dp'=4,'fsdp'=8] {'dp','fsdp'}, use_global_device_ids=true, to_apply=%region_12.13.clone | all-reduce | flops 4096 | bytes 32768
  907.9 323.1 %all-reduce.9.cloned.1.call-done = bf16[1408,2,2048]{2,1,0:T(2,128)(2,1)} async-done(((bf16[1408,2,2048]{2,1,0:T(2,128)(2,1)}), bf16[1408,2,2048]{2,1,0:T(2,128)(2,1)}) %all-reduce.9.cloned.1.call-update) | async-done | bytes 11534352
  1231.0 4.6 dynamic-slice_convert_fusion
  1235.7 207.4 %reduce-scatter.10.cloned.1.call-done = f32[64,2304]{1,0:T(8,128)} async-done(((f32[2048,2304]{1,0:T(8,128)}), f32[64,2304]{1,0:T(8,128)}) %reduce-scatter.10.cloned.1.call-update) | async-done | bytes 589840 | tf_op jit(solution)/shard_map/reduce_scatter | solution.py:216
  1446.4 356.5 %reduce-scatter.12.cloned.1.call-done = f32[64,2048]{1,0:T(8,128)} async-done(((f32[2048,2048]{1,0:T(8,128)}), f32[64,2048]{1,0:T(8,128)}) %reduce-scatter.12.cloned.1.call-update) | async-done | bytes 524304 | tf_op jit(solution)/shard_map/reduce_scatter | solution.py:180
  (175 shorter events, 96.7 us)
Async XLA Ops:
  7.2 48.7 %copy-start.1 = (bf16[256,2048]{1,0:T(8,128)(2,1)S(1)}, bf16[256,2048]{1,0:T(8,128)(2,1)}, u32[]{:S(2)}) copy-start(bf16[256,2048]{1,0:T(8,128)(2,1)} %param.13) | copy-start | bytes 3145732
  7.2 60.6 %all-gather.8.cloned.1.call-start = ((), (), s32[]{:S(2)}) async-start(), calls=%async_computation.5 | async-start | bytes 1081344 | tf_op jit(solution)/shard_map/all_gather | solution.py:85
  7.9 139.1 %all-gather.10.cloned.1.call-start = ((), (), s32[]{:S(2)}) async-start(), calls=%async_computation.6 | async-start | bytes 8650752 | tf_op jit(solution)/shard_map/all_gather | solution.py:84
  8.7 217.4 %all-gather.12.cloned.1.call-start = ((), (), s32[]{:S(2)}) async-start(), calls=%async_computation.7 | async-start | bytes 8650752 | tf_op jit(solution)/shard_map/all_gather | solution.py:117
  9.4 381.5 %all-gather.16.cloned.1.call-start = ((), (), s32[]{:S(2)}) async-start(), calls=%async_computation.9 | async-start | bytes 12976128 | tf_op jit(solution)/shard_map/all_gather | solution.py:130
  12.5 413.1 %all-gather.14.cloned.1.call-start = ((), (), s32[]{:S(2)}) async-start(), calls=%async_computation.8 | async-start | bytes 5242880 | tf_op jit(solution)/shard_map/all_gather | solution.py:127
  55.2 91.8 %copy-start.14 = (f32[2048]{0:T(1024)}, f32[2048]{0:T(1024)S(1)}, u32[]{:S(2)}) copy-start(f32[2048]{0:T(1024)S(1)} %convert_element_type.95) | copy-start | bytes 24580
  55.8 14.3 copy-start.28
  56.2 90.9 %copy-start.24 = (f32[256]{0:T(256)}, f32[256]{0:T(256)S(1)}, u32[]{:S(2)}) copy-start(f32[256]{0:T(256)S(1)} %add_rsqrt_fusion.1) | copy-start | bytes 3076
  69.6 77.4 %copy-start.12 = (f32[256,256]{0,1:T(8,128)}, f32[256,256]{0,1:T(8,128)S(1)}, u32[]{:S(2)}) copy-start(f32[256,256]{0,1:T(8,128)S(1)} %fusion.81) | copy-start | bytes 786436
  70.0 85.3 %copy-start.16 = (bf16[256,64]{0,1:T(8,128)(2,1)}, bf16[256,64]{0,1:T(8,128)(2,1)S(1)}, u32[]{:S(2)}) copy-start(bf16[256,64]{0,1:T(8,128)(2,1)S(1)} %get-tuple-element.63) | copy-start | bytes 98308
  70.0 85.3 %copy-start.18 = (bf16[256,64]{0,1:T(8,128)(2,1)}, bf16[256,64]{0,1:T(8,128)(2,1)S(1)}, u32[]{:S(2)}) copy-start(bf16[256,64]{0,1:T(8,128)(2,1)S(1)} %get-tuple-element.64) | copy-start | bytes 98308
  226.1 6.2 copy-start.21
  232.3 212.5 %copy-start.27 = (f32[256]{0:T(256)}, f32[256]{0:T(256)S(1)}, u32[]{:S(2)}) copy-start(f32[256]{0:T(256)S(1)} %add_rsqrt_fusion) | copy-start | bytes 3076
  233.5 228.6 %all-gather.18.cloned.1.call-start = ((), (), s32[]{:S(2)}) async-start(), calls=%async_computation.11 | async-start | bytes 5242880 | tf_op jit(solution)/shard_map/all_gather | solution.py:128
  238.1 318.9 %all-gather.20.cloned.1.call-start = ((), (), s32[]{:S(2)}) async-start(), calls=%async_computation.12 | async-start | bytes 6488064 | tf_op jit(solution)/shard_map/all_gather | solution.py:144
  238.8 538.4 %reduce-scatter.8.cloned.1.call-start = ((), (), s32[]{:S(2)}) async-start(), calls=%async_computation.13 | async-start | bytes 5242880 | tf_op jit(solution)/shard_map/reduce_scatter | solution.py:154
  591.4 188.5 %reduce-scatter.6.cloned.1.call-start = ((), (), s32[]{:S(2)}) async-start(), calls=%async_computation.10 | async-start | bytes 5242880 | tf_op jit(solution)/shard_map/reduce_scatter | solution.py:140
  591.5 31.5 %collective-permute-start = (bf16[176,2048]{1,0:T(8,128)(2,1)}, bf16[176,2048]{1,0:T(8,128)(2,1)}, u32[]{:S(2)}, u32[]{:S(2)}) collective-permute-start(bf16[176,2048]{1,0:T(8,128)(2,1)} %param.20), channel_id=1, source_target_pairs={{0,1},{1,2},{2,3},{3,4},{4,5},{5,6},{6,7},{7,0},{8,9},{9,10},{10,1... | collective-permute-start | bytes 2162696 | tf_op jit(solution)/shard_map/ppermute | solution.py:18
  592.5 33.0 %collective-permute-start.1 = (bf16[176,2048]{1,0:T(8,128)(2,1)}, bf16[176,2048]{1,0:T(8,128)(2,1)}, u32[]{:S(2)}, u32[]{:S(2)}) collective-permute-start(bf16[176,2048]{1,0:T(8,128)(2,1)} %param.20), channel_id=1, source_target_pairs={{0,7},{1,0},{2,1},{3,2},{4,3},{5,4},{6,5},{7,6},{8,15},{9,8},{10,9... | collective-permute-start | bytes 2162696 | tf_op jit(solution)/shard_map/ppermute | solution.py:21
  622.9 32.3 %collective-permute-start.2 = (bf16[176,2048]{1,0:T(8,128)(2,1)}, bf16[176,2048]{1,0:T(8,128)(2,1)}, u32[]{:S(2)}, u32[]{:S(2)}) collective-permute-start(bf16[176,2048]{1,0:T(8,128)(2,1)} %collective-permute-done), channel_id=1, source_target_pairs={{0,1},{1,2},{2,3},{3,4},{4,5},{5,6},{6,7},{7,0},{8,9},{9,10},{10,1... | collective-permute-start | bytes 2162696 | tf_op jit(solution)/shard_map/ppermute | solution.py:18
  625.4 34.9 %collective-permute-start.3 = (bf16[176,2048]{1,0:T(8,128)(2,1)}, bf16[176,2048]{1,0:T(8,128)(2,1)S(1)}, u32[]{:S(2)}, u32[]{:S(2)}) collective-permute-start(bf16[176,2048]{1,0:T(8,128)(2,1)} %collective-permute-done.1), channel_id=1, source_target_pairs={{0,7},{1,0},{2,1},{3,2},{4,3},{5,4},{6,5},{7,6},{8,15},{9,8},{10,9... | collective-permute-start | bytes 2162696 | tf_op jit(solution)/shard_map/ppermute | solution.py:21
  655.3 32.3 %collective-permute-start.4 = (bf16[176,2048]{1,0:T(8,128)(2,1)}, bf16[176,2048]{1,0:T(8,128)(2,1)S(1)}, u32[]{:S(2)}, u32[]{:S(2)}) collective-permute-start(bf16[176,2048]{1,0:T(8,128)(2,1)} %collective-permute-done.2), channel_id=1, source_target_pairs={{0,1},{1,2},{2,3},{3,4},{4,5},{5,6},{6,7},{7,0},{8,9},{9,10},{10,1... | collective-permute-start | bytes 2162696 | tf_op jit(solution)/shard_map/ppermute | solution.py:18
  658.9 47.1 %copy-start.34 = (bf16[1024,1408]{1,0:T(8,128)(2,1)S(1)}, bf16[1024,1408]{1,0:T(8,128)(2,1)}, u32[]{:S(2)}) copy-start(bf16[1024,1408]{1,0:T(8,128)(2,1)} %get-tuple-element.54) | copy-start | bytes 8650756
  660.3 30.2 %collective-permute-start.5 = (bf16[176,2048]{1,0:T(8,128)(2,1)S(1)}, bf16[176,2048]{1,0:T(8,128)(2,1)S(1)}, u32[]{:S(2)}, u32[]{:S(2)}) collective-permute-start(bf16[176,2048]{1,0:T(8,128)(2,1)S(1)} %collective-permute-done.3), channel_id=1, source_target_pairs={{0,7},{1,0},{2,1},{3,2},{4,3},{5,4},{6,5},{7,6},{8,15},{9,8},{10,9... | collective-permute-start | bytes 2162696 | tf_op jit(solution)/shard_map/ppermute | solution.py:21
  687.6 18.3 %collective-permute-start.6 = (bf16[176,2048]{1,0:T(8,128)(2,1)S(1)}, bf16[176,2048]{1,0:T(8,128)(2,1)S(1)}, u32[]{:S(2)}, u32[]{:S(2)}) collective-permute-start(bf16[176,2048]{1,0:T(8,128)(2,1)S(1)} %collective-permute-done.4), channel_id=1, source_target_pairs={{0,1},{1,2},{2,3},{3,4},{4,5},{5,6},{6,7},{7,0},{8,9},{9,10},{10,1... | collective-permute-start | bytes 2162696 | tf_op jit(solution)/shard_map/ppermute | solution.py:18
  714.3 191.2 %reduce-scatter.14.cloned.1.call-start = ((), (), s32[]{:S(2)}) async-start(), calls=%async_computation.16 | async-start | bytes 6488064 | tf_op jit(solution)/shard_map/reduce_scatter | solution.py:157
  725.0 506.1 %all-reduce.9.cloned.1.call-start = ((), (), s32[]{:S(2)}) async-start(), calls=%async_computation.17 | async-start | bytes 23068672
  772.7 670.4 %reduce-scatter.10.cloned.1.call-start = ((), (), s32[]{:S(2)}) async-start(), calls=%async_computation.14 | async-start | bytes 19464192 | tf_op jit(solution)/shard_map/reduce_scatter | solution.py:216
  775.9 21.9 %copy-start.10 = (f32[256,256]{0,1:T(8,128)}, f32[256,256]{0,1:T(8,128)S(1)}, u32[]{:S(2)}) copy-start(f32[256,256]{0,1:T(8,128)S(1)} %convert_multiply_fusion.5) | copy-start | bytes 786436
  824.0 12.3 copy-start.7
  836.3 966.6 %reduce-scatter.12.cloned.1.call-start = ((), (), s32[]{:S(2)}) async-start(), calls=%async_computation.15 | async-start | bytes 17301504 | tf_op jit(solution)/shard_map/reduce_scatter | solution.py:180
  (25 other events, 77.2 us)
Sparse Core Ops, SparseCore 0:
  11.1 56.5 all-gather.7
  70.7 76.2 all-gather.9
  150.0 75.9 all-gather.11
  228.7 162.2 all-gather.15
  392.9 32.6 all-gather.13
  427.6 34.4 all-gather.17
  464.3 92.6 all-gather.19
  591.5 42.6 reduce-scatter.7
  714.5 42.7 reduce-scatter.5
  760.8 109.9 reduce-scatter.13
  874.7 356.3 all-reduce.8
  1237.3 205.7 reduce-scatter.9
  1445.9 356.9 reduce-scatter.11
